TPU v7x, 256 devices: a whole 4x4x8 slice. The times are simulated.
256 devices in a mesh: dp: 32 (over z, y), block: 8 (over x, core).
Axes of the slice: x: 4, y: 4, z: 8, core: 2. Of those that a mesh axis runs over, the one named last changes fastest.
Arguments:
- x_act: bfloat16 [8, 16384, 4096], P('block', 'dp')
- g_out: bfloat16 [8, 16384, 4096], P('block', 'dp')
- proj_in: bfloat16 [8, 4096, 64], P('block'), may hold values from -0.09375 to 0.09375
- proj_out: bfloat16 [8, 4096, 64], P('block'), may hold values from -0.09375 to 0.09375
- queries: bfloat16 [8, 2048, 4096], P('block', 'dp'), may hold values from -6 to 6
- cand_ids: int32 [32, 32, 2], P('dp'), may hold values from 0 to 15, as said below
- cand_counts: int32 [32, 32], P('dp'), may hold values from 0 to 2, as said below
Outputs:
- scores: float32 [2048, 128], P(('dp', 'block'))
Inputs may be any that keep to these rules, and one draw needn't show every extreme that they name: `cand_ids`: each list of a training shard d for an owner p names 2 distinct query blocks of p; slots at or past cand_counts[d, p] are padding. Every training shard d has cand_counts[d, d] = 2.
All inputs are finite; a program needn't handle non-finite values.
Results may differ from a plain program's by a relative error of at most 0.0096.
Values may be sent and summed in bfloat16 or wider, within the bound.
No kernel may reach another device: no remote copies, remote signals or barrier semaphores. Data moves between devices by JAX's collectives and lax.ppermute only.
A program may use at most 64 MiB of HBM per device.

v0:
```python
import jax
import jax.numpy as jnp
from jax import lax
from jax.sharding import PartitionSpec as P

E_DEV = 4
SEQ = 128
QB = 4
CAP = 2
DAMP = 0.1


def kron_inverse(factor):
    width = factor.shape[0]
    identity = jnp.eye(width, dtype=jnp.float32)
    damping = DAMP * jnp.trace(factor) / width + 1e-06
    lower_factor = jnp.linalg.cholesky(factor + damping * identity)
    return jax.scipy.linalg.cho_solve((lower_factor, True), identity)


def body(x_act, g_out, proj_in, proj_out, queries, cand_ids, cand_counts):
    act_rows = x_act[0]
    grad_rows = g_out[0]
    row_count = act_rows.shape[0]
    width = proj_in.shape[2]
    n_owners = lax.axis_size("dp")
    n_layers = lax.axis_size("block")
    act_proj = jnp.dot(act_rows, proj_in[0], preferred_element_type=jnp.float32).astype(
        jnp.bfloat16
    )
    grad_proj = jnp.dot(grad_rows, proj_out[0], preferred_element_type=jnp.float32).astype(
        jnp.bfloat16
    )
    contract_rows = (((0,), (0,)), ((), ()))
    part_a = lax.dot_general(act_proj, act_proj, contract_rows, preferred_element_type=jnp.float32)
    part_g = lax.dot_general(
        grad_proj, grad_proj, contract_rows, preferred_element_type=jnp.float32
    )
    factor_a, factor_g = lax.psum((part_a, part_g), "dp")
    token_total = row_count * n_owners
    inverse_a = kron_inverse(factor_a / token_total)
    inverse_g = kron_inverse(factor_g / token_total)
    act_three = act_proj.reshape(E_DEV, SEQ, width)
    grad_three = grad_proj.reshape(E_DEV, SEQ, width)
    example_grad = (
        jnp.einsum("esi,esj->eij", grad_three, act_three, preferred_element_type=jnp.float32) / SEQ
    )
    left_side = jnp.einsum("ij,ejk->eik", inverse_g, example_grad, precision=lax.Precision.HIGHEST)
    precond = jnp.einsum("eik,kl->eil", left_side, inverse_a, precision=lax.Precision.HIGHEST)
    precond = precond.reshape(E_DEV, width * width).astype(jnp.bfloat16)
    req_ids, req_counts = (
        lax.all_to_all(cand_ids, "dp", split_axis=1, concat_axis=0, tiled=True),
        lax.all_to_all(cand_counts, "dp", split_axis=1, concat_axis=0, tiled=True),
    )
    req_ids = req_ids.reshape(n_owners, CAP)
    req_counts = req_counts.reshape(n_owners)
    query_rows = queries[0]
    owned = query_rows.shape[0]
    block_count = owned // QB
    slot_live = jnp.arange(CAP)[None, :] < req_counts[:, None]
    onehot = (
        (req_ids[:, :, None] == jnp.arange(block_count)[None, None, :]) & slot_live[:, :, None]
    ).astype(jnp.float32)
    dense_part = lax.dot_general(
        query_rows,
        lax.all_gather(precond, "dp", axis=0, tiled=True),
        (((1,), (1,)), ((), ())),
        preferred_element_type=jnp.float32,
    )
    live_blocks = jnp.sum(onehot, axis=1)
    mask_full = jnp.broadcast_to(
        jnp.transpose(live_blocks)[:, None, :, None], (block_count, QB, n_owners, E_DEV)
    ).reshape(owned, n_owners * E_DEV)
    layer_part = dense_part * mask_full
    scale = 1.0 / float(width * width * n_layers) ** 0.5
    return lax.psum_scatter(layer_part * scale, "block", scatter_dimension=0, tiled=True)


def solution(mesh):
    return jax.shard_map(
        body,
        mesh=mesh,
        in_specs=(
            P("block", "dp", None),
            P("block", "dp", None),
            P("block", None, None),
            P("block", None, None),
            P("block", "dp", None),
            P("dp", None, None),
            P("dp", None),
        ),
        out_specs=P(("dp", "block"), None),
        check_vma=False,
    )
```

profile of v0, /device:TPU:64, one launch (start us, length us, event | category | flops | bytes accessed | tf_op | source)
XLA Modules:
  0.0 291.4 jit_solution(2975817334751202043)
XLA Ops:
  6.5 1.0 copy-done
  7.6 3.7 %fusion.4 = bf16[512,64]{0,1:T(8,128)(2,1)S(1)} fusion(bf16[1,512,4096]{2,1,0:T(8,128)(2,1)} %param.11, bf16[1,4096,64]{1,2,0:T(8,128)(2,1)S(1)} %copy-done), kind=kOutput, calls=%fused_computation.6 | convolution fusion | flops 268468224 | bytes 4784128 | tf_op jit(solution)/shard_map/dot_general | solution.py:31
  11.5 1.4 fusion.7
  13.2 133.0 %all-reduce.1 = (f32[64,64]{0,1:T(8,128)S(1)}, f32[64,64]{0,1:T(8,128)S(1)}) all-reduce(f32[64,64]{0,1:T(8,128)S(1)} %fusion.32, f32[64,64]{0,1:T(8,128)S(1)} %fusion.33), channel_id=1, replica_groups=mesh['dp'=32,'block'=8] {'dp'}, use_global_device_ids=true, to_apply=%region_0.0 | all-reduce | flops 8192 | bytes 65536 | tf_op jit(solution)/shard_map/psum | solution.py:39
  146.2 0.7 select_reduce_fusion.3
  149.0 5.8 %cholesky.55 = f32[64,64]{1,0:T(8,128)S(1)} custom-call(f32[64,64]{1,0:T(8,128)S(1)} %fusion.27), custom_call_target="Cholesky" | custom-call | tf_op jit(solution)/shard_map/jit(cholesky)/cholesky | solution.py:17
  154.9 0.6 compare_reduce_fusion
  155.5 0.7 fusion.24
  156.2 4.9 %custom-call.9 = f32[1,64,64]{1,2,0:T(8,128)S(1)} custom-call(f32[1,64,64]{2,1,0:T(8,128)S(1)} %fusion.24), custom_call_target="InvertDiagBlocksLowerTriangular" | custom-call | tf_op jit(solution)/shard_map/jit(_cho_solve)/triangular_solve | solution.py:18
  161.6 5.8 %cholesky.44 = f32[64,64]{1,0:T(8,128)S(1)} custom-call(f32[64,64]{1,0:T(8,128)S(1)} %fusion.30), custom_call_target="Cholesky" | custom-call | tf_op jit(solution)/shard_map/jit(cholesky)/cholesky | solution.py:17
  168.1 0.7 fusion.23
  168.8 4.9 %custom-call.8 = f32[1,64,64]{1,2,0:T(8,128)S(1)} custom-call(f32[1,64,64]{2,1,0:T(8,128)S(1)} %fusion.23), custom_call_target="InvertDiagBlocksLowerTriangular" | custom-call | tf_op jit(solution)/shard_map/jit(_cho_solve)/triangular_solve | solution.py:18
  174.9 0.7 reshape.60
  175.6 0.7 copy.52
  176.3 16.2 %all-to-all-start.1 = ((s32[1,32,1]{2,0,1:T(1,128)}), s32[1,32,1]{2,0,1:T(1,128)S(1)}, u32[]{:S(2)}, u32[]{:S(2)}) async-start(s32[1,32,1]{2,0,1:T(1,128)} %copy.52), calls=%async_computation.1 | async-start | bytes 32768 | tf_op jit(solution)/shard_map/all_to_all | solution.py:53
  192.5 0.7 copy.50
  194.4 5.8 %all-to-all-done.1 = s32[1,32,1]{2,0,1:T(1,128)S(1)} async-done(((s32[1,32,1]{2,0,1:T(1,128)}), s32[1,32,1]{2,0,1:T(1,128)S(1)}, u32[]{:S(2)}, u32[]{:S(2)}) %all-to-all-start.1) | async-done | bytes 160 | tf_op jit(solution)/shard_map/all_to_all | solution.py:53
  200.3 5.6 %all-to-all-start = ((s32[1,32,2]{2,0,1:T(1,128)}), s32[1,32,2]{2,0,1:T(1,128)S(1)}, u32[]{:S(2)}, u32[]{:S(2)}) async-start(s32[1,32,2]{2,0,1:T(1,128)} %copy.50), calls=%async_computation | async-start | bytes 32768 | tf_op jit(solution)/shard_map/all_to_all | solution.py:52
  205.9 0.7 reduce.4
  206.5 7.1 %all-to-all-done = s32[1,32,2]{2,0,1:T(1,128)S(1)} async-done(((s32[1,32,2]{2,0,1:T(1,128)}), s32[1,32,2]{2,0,1:T(1,128)S(1)}, u32[]{:S(2)}, u32[]{:S(2)}) %all-to-all-start) | async-done | bytes 288 | tf_op jit(solution)/shard_map/all_to_all | solution.py:52
  213.9 0.6 reshape.59
  214.6 43.9 %all-gather.3.cloned.1.call-done = bf16[32,4,4096]{2,1,0:T(4,128)(2,1)} async-done(((bf16[1,4,4096]{2,1,0:T(4,128)(2,1)}), bf16[32,4,4096]{2,1,0:T(4,128)(2,1)}) %all-gather.3.cloned.1.call-update) | async-done | bytes 1048592 | tf_op jit(solution)/shard_map/all_gather | solution.py:66
  258.5 1.3 reshape.61
  260.4 23.6 %all-reduce = f32[64,128]{1,0:T(8,128)S(1)} all-reduce(f32[64,128]{1,0:T(8,128)S(1)} %fusion.11), channel_id=2, replica_groups=mesh['dp'=32,'block'=8] {'block'}, use_global_device_ids=true, to_apply=%region_7.10.clone | all-reduce | flops 8192 | bytes 65536
  (40 shorter events, 5.5 us)
Async XLA Ops:
  6.5 1.0 copy-start
  6.5 5.0 %copy-start.2 = (bf16[1,4096,64]{1,2,0:T(8,128)(2,1)S(1)}, bf16[1,4096,64]{1,2,0:T(8,128)(2,1)}, u32[]{:S(2)}) copy-start(bf16[1,4096,64]{1,2,0:T(8,128)(2,1)} %param.12) | copy-start | bytes 1572868
  6.5 252.0 %all-gather.3.cloned.1.call-start = ((), (), s32[]{:S(2)}) async-start(), calls=%async_computation.2 | async-start | bytes 1081344 | tf_op jit(solution)/shard_map/all_gather | solution.py:66
  7.6 3.9 %copy-start.1 = (bf16[1,512,4096]{2,1,0:T(8,128)(2,1)S(1)}, bf16[1,512,4096]{2,1,0:T(8,128)(2,1)}, u32[]{:S(2)}) copy-start(bf16[1,512,4096]{2,1,0:T(8,128)(2,1)} %param.10) | copy-start | bytes 12582916
  11.3 164.3 %copy-start.5 = (s32[1,32]{1,0:T(1,128)S(1)}, s32[1,32]{1,0:T(1,128)}, u32[]{:S(2)}) copy-start(s32[1,32]{1,0:T(1,128)} %param.16) | copy-start | bytes 388
  11.3 181.2 %copy-start.4 = (s32[1,32,2]{1,2,0:T(2,128)S(1)}, s32[1,32,2]{1,2,0:T(2,128)}, u32[]{:S(2)}) copy-start(s32[1,32,2]{1,2,0:T(2,128)} %param.15) | copy-start | bytes 772
  11.3 181.9 %copy-start.6 = (u32[256]{0:T(256)S(1)}, u32[256]{0:T(256)}, u32[]{:S(2)}) copy-start(u32[256]{0:T(256)} %constant.72) | copy-start | bytes 3076
  12.9 247.0 %copy-start.3 = (bf16[1,64,4096]{2,1,0:T(8,128)(2,1)S(1)}, bf16[1,64,4096]{2,1,0:T(8,128)(2,1)}, u32[]{:S(2)}) copy-start(bf16[1,64,4096]{2,1,0:T(8,128)(2,1)} %param.14) | copy-start | bytes 1572868
  176.3 24.0 %all-to-all-start.1 = ((s32[1,32,1]{2,0,1:T(1,128)}), s32[1,32,1]{2,0,1:T(1,128)S(1)}, u32[]{:S(2)}, u32[]{:S(2)}) async-start(s32[1,32,1]{2,0,1:T(1,128)} %copy.52), calls=%async_computation.1 | async-start | bytes 32768 | tf_op jit(solution)/shard_map/all_to_all | solution.py:53
  200.3 13.4 %all-to-all-start = ((s32[1,32,2]{2,0,1:T(1,128)}), s32[1,32,2]{2,0,1:T(1,128)S(1)}, u32[]{:S(2)}, u32[]{:S(2)}) async-start(s32[1,32,2]{2,0,1:T(1,128)} %copy.50), calls=%async_computation | async-start | bytes 32768 | tf_op jit(solution)/shard_map/all_to_all | solution.py:52
Sparse Core Ops, SparseCore 0:
  175.7 82.7 all-gather.2
where the time goes:
time: 292 us; the launch traced here: 291 us
  blocking collectives  157 us (54%)
  waiting for transfers between devices  56.9 us (19%)
  other arithmetic  26.1 us (9%)
  starting transfers between devices  21.8 us (7%)
  between operations  15.6 us (5%)
  matrix products  7.64 us (3%)
  local copies, waits for them, and re-layouts  6.72 us (2%)
    psum x1, blocking collectives, body(): factor_a, factor_g = lax.psum((part_a, part_g), 'dp')  133 us
    all_gather x1, waiting for transfers between devices, body(): lax.all_gather(precond, 'dp', axis=0, tiled=True)  43.9 us
    unnamed x1, blocking collectives  23.6 us
    all_to_all x1, starting transfers between devices, body(): lax.all_to_all(cand_counts, 'dp', split_axis=1, concat_axis=0, tiled=True)  16.2 us
    another operation x6, other arithmetic, kron_inverse(): lower_factor = jnp.linalg.cholesky(factor + damping * identity)  13 us
    another operation x4, other arithmetic, kron_inverse(): return jax.scipy.linalg.cho_solve((lower_factor, True), identity)  11.1 us
    all_to_all x1, waiting for transfers between devices, body(): lax.all_to_all(cand_ids, 'dp', split_axis=1, concat_axis=0, tiled=True)  7.09 us
  transfers between devices with their start and end apart: 3, of which 3 were waited for; matrix products, arithmetic and copies ran while one was open for 1% of the time, Pallas kernels for 0%

commit v1 on v0

--- a/solution.py
+++ b/solution.py
@@ -8,6 +8,12 @@
 QB = 4
 CAP = 2
 DAMP = 0.1
+
+
+def tiled_gather(x, axis, dim):
+    devices = lax.axis_size(axis)
+    repeats = [devices if d == dim else 1 for d in range(x.ndim)]
+    return lax.all_to_all(jnp.tile(x, repeats), axis, split_axis=dim, concat_axis=dim, tiled=True)
 
 
 def kron_inverse(factor):
@@ -63,7 +69,7 @@
     ).astype(jnp.float32)
     dense_part = lax.dot_general(
         query_rows,
-        lax.all_gather(precond, "dp", axis=0, tiled=True),
+        tiled_gather(precond, "dp", 0),
         (((1,), (1,)), ((), ())),
         preferred_element_type=jnp.float32,
     )

time: 292 us -> 254 us (0.87)
  waiting for transfers between devices: 56.9 us -> 22.7 us
  between operations: 15.6 us -> 2.13 us
  starting transfers between devices: 21.8 us -> 34.1 us
  blocking collectives: 157 us -> 154 us
    all_gather x1 -> x0, waiting for transfers between devices: 43.9 us -> none  [body(): lax.all_gather(precond, 'dp', axis=0, tiled=True)]
    all_to_all x0 -> x1, waiting for transfers between devices: none -> 15.5 us  [tiled_gather(): lax.all_to_all(jnp.tile(x, repeats), axis, split_axis=dim, concat_axis=di...]
    all_to_all x1, starting transfers between devices: 5.59 us -> 17.3 us  [body(): lax.all_to_all(cand_ids, 'dp', split_axis=1, concat_axis=0, tiled=True)]
    all_to_all x0 -> x1, starting transfers between devices: none -> 5.91 us  [tiled_gather(): lax.all_to_all(jnp.tile(x, repeats), axis, split_axis=dim, concat_axis=di...]
    all_to_all x1, waiting for transfers between devices: 5.84 us -> 0.01 us  [body(): lax.all_to_all(cand_counts, 'dp', split_axis=1, concat_axis=0, tiled=True)]
    all_to_all x1, starting transfers between devices: 16.2 us -> 10.9 us  [body(): lax.all_to_all(cand_counts, 'dp', split_axis=1, concat_axis=0, tiled=True)]
    unnamed x19 -> x15, local copies, waits for them, and re-layouts: 4.98 us -> 1.9 us
  transfers between devices with their start and end apart: 3 -> 3, of which waited for: 3 -> 2; matrix products, arithmetic and copies ran while one was open for 1% -> 14% of each run, Pallas kernels for 0% -> 0%
where the time goes in v1:
time: 254 us; the launch traced here: 253 us
  blocking collectives  154 us (61%)
  starting transfers between devices  34.1 us (13%)
  other arithmetic  26.1 us (10%)
  waiting for transfers between devices  22.7 us (9%)
  matrix products  7.65 us (3%)
  local copies, waits for them, and re-layouts  6.21 us (2%)
    psum x1, blocking collectives, body(): factor_a, factor_g = lax.psum((part_a, part_g), 'dp')  130 us
    unnamed x1, blocking collectives  23.6 us
    all_to_all x1, starting transfers between devices, body(): lax.all_to_all(cand_ids, 'dp', split_axis=1, concat_axis=0, tiled=True)  17.3 us
    all_to_all x1, waiting for transfers between devices, tiled_gather(): lax.all_to_all(jnp.tile(x, repeats), axis, split_axis=dim, concat_axis=di...  15.5 us
    another operation x6, other arithmetic, kron_inverse(): lower_factor = jnp.linalg.cholesky(factor + damping * identity)  13 us
    another operation x4, other arithmetic, kron_inverse(): return jax.scipy.linalg.cho_solve((lower_factor, True), identity)  11.1 us
    all_to_all x1, starting transfers between devices, body(): lax.all_to_all(cand_counts, 'dp', split_axis=1, concat_axis=0, tiled=True)  10.9 us
    all_to_all x1, waiting for transfers between devices, body(): lax.all_to_all(cand_ids, 'dp', split_axis=1, concat_axis=0, tiled=True)  7.19 us
  transfers between devices with their start and end apart: 3, of which 2 were waited for; matrix products, arithmetic and copies ran while one was open for 14% of the time, Pallas kernels for 0%

profile of v1, /device:TPU:64, one launch (start us, length us, event | category | flops | bytes accessed | tf_op | source)
XLA Modules:
  0.0 253.0 jit_solution(6339354013856781801)
XLA Ops:
  0.0 1.4 copy.52
  1.4 10.9 %all-to-all-start.2 = ((s32[1,32,1]{2,0,1:T(1,128)}), s32[1,32,1]{2,0,1:T(1,128)S(1)}, u32[]{:S(2)}, u32[]{:S(2)}) async-start(s32[1,32,1]{2,0,1:T(1,128)} %copy.52), calls=%async_computation.2 | async-start | bytes 32768 | tf_op jit(solution)/shard_map/all_to_all | solution.py:59
  12.4 3.7 %fusion.4 = bf16[512,64]{0,1:T(8,128)(2,1)S(1)} fusion(bf16[1,512,4096]{2,1,0:T(8,128)(2,1)} %param.11, bf16[1,4096,64]{1,2,0:T(8,128)(2,1)S(1)} %copy-done), kind=kOutput, calls=%fused_computation.6 | convolution fusion | flops 268468224 | bytes 4784128 | tf_op jit(solution)/shard_map/dot_general | solution.py:37
  16.3 1.4 fusion.7
  18.0 130.5 %all-reduce.1 = (f32[64,64]{0,1:T(8,128)S(1)}, f32[64,64]{0,1:T(8,128)S(1)}) all-reduce(f32[64,64]{0,1:T(8,128)S(1)} %fusion.32, f32[64,64]{0,1:T(8,128)S(1)} %fusion.33), channel_id=1, replica_groups=mesh['dp'=32,'block'=8] {'dp'}, use_global_device_ids=true, to_apply=%region_0.0 | all-reduce | flops 8192 | bytes 65536 | tf_op jit(solution)/shard_map/psum | solution.py:45
  148.5 0.6 select_reduce_fusion.3
  149.1 0.6 select_reduce_fusion.2
  151.0 5.8 %cholesky.55 = f32[64,64]{1,0:T(8,128)S(1)} custom-call(f32[64,64]{1,0:T(8,128)S(1)} %fusion.27), custom_call_target="Cholesky" | custom-call | tf_op jit(solution)/shard_map/jit(cholesky)/cholesky | solution.py:23
  156.9 0.6 compare_reduce_fusion
  157.5 0.7 fusion.24
  158.2 4.9 %custom-call.9 = f32[1,64,64]{1,2,0:T(8,128)S(1)} custom-call(f32[1,64,64]{2,1,0:T(8,128)S(1)} %fusion.24), custom_call_target="InvertDiagBlocksLowerTriangular" | custom-call | tf_op jit(solution)/shard_map/jit(_cho_solve)/triangular_solve | solution.py:24
  163.4 5.8 %cholesky.44 = f32[64,64]{1,0:T(8,128)S(1)} custom-call(f32[64,64]{1,0:T(8,128)S(1)} %fusion.30), custom_call_target="Cholesky" | custom-call | tf_op jit(solution)/shard_map/jit(cholesky)/cholesky | solution.py:23
  169.3 0.6 compare_reduce_fusion.1
  170.0 0.7 fusion.23
  170.6 4.9 %custom-call.8 = f32[1,64,64]{1,2,0:T(8,128)S(1)} custom-call(f32[1,64,64]{2,1,0:T(8,128)S(1)} %fusion.23), custom_call_target="InvertDiagBlocksLowerTriangular" | custom-call | tf_op jit(solution)/shard_map/jit(_cho_solve)/triangular_solve | solution.py:24
  176.5 0.7 copy.50
  177.2 17.3 %all-to-all-start.1 = ((s32[1,32,2]{2,0,1:T(1,128)}), s32[1,32,2]{2,0,1:T(1,128)S(1)}, u32[]{:S(2)}, u32[]{:S(2)}) async-start(s32[1,32,2]{2,0,1:T(1,128)} %copy.50), calls=%async_computation.1 | async-start | bytes 32768 | tf_op jit(solution)/shard_map/all_to_all | solution.py:58
  195.0 7.2 %all-to-all-done.1 = s32[1,32,2]{2,0,1:T(1,128)S(1)} async-done(((s32[1,32,2]{2,0,1:T(1,128)}), s32[1,32,2]{2,0,1:T(1,128)S(1)}, u32[]{:S(2)}, u32[]{:S(2)}) %all-to-all-start.1) | async-done | bytes 288 | tf_op jit(solution)/shard_map/all_to_all | solution.py:58
  202.2 1.5 tile.2
  203.7 5.9 %all-to-all-start = ((bf16[32,4,4096]{2,1,0:T(4,128)(2,1)}), bf16[32,4,4096]{2,1,0:T(4,128)(2,1)S(1)}, u32[]{:S(2)}, u32[]{:S(2)}) async-start(bf16[32,4,4096]{2,1,0:T(4,128)(2,1)} %tile.2), calls=%async_computation | async-start | bytes 2097152 | tf_op jit(solution)/shard_map/all_to_all | solution.py:16
  210.9 0.7 reduce.4
  211.8 0.6 reshape.70
  212.5 15.5 %all-to-all-done = bf16[32,4,4096]{2,1,0:T(4,128)(2,1)S(1)} async-done(((bf16[32,4,4096]{2,1,0:T(4,128)(2,1)}), bf16[32,4,4096]{2,1,0:T(4,128)(2,1)S(1)}, u32[]{:S(2)}, u32[]{:S(2)}) %all-to-all-start) | async-done | bytes 1048608 | tf_op jit(solution)/shard_map/all_to_all | solution.py:16
  228.8 23.6 %all-reduce = f32[64,128]{1,0:T(8,128)S(1)} all-reduce(f32[64,128]{1,0:T(8,128)S(1)} %fusion.11), channel_id=2, replica_groups=mesh['dp'=32,'block'=8] {'block'}, use_global_device_ids=true, to_apply=%region_7.10.clone | all-reduce | flops 8192 | bytes 65536
  (38 shorter events, 4.7 us)
Async XLA Ops:
  0.0 12.3 %copy-start = (bf16[1,4096,64]{1,2,0:T(8,128)(2,1)S(1)}, bf16[1,4096,64]{1,2,0:T(8,128)(2,1)}, u32[]{:S(2)}) copy-start(bf16[1,4096,64]{1,2,0:T(8,128)(2,1)} %param.13) | copy-start | bytes 1572868
  0.0 16.3 %copy-start.2 = (bf16[1,4096,64]{1,2,0:T(8,128)(2,1)S(1)}, bf16[1,4096,64]{1,2,0:T(8,128)(2,1)}, u32[]{:S(2)}) copy-start(bf16[1,4096,64]{1,2,0:T(8,128)(2,1)} %param.12) | copy-start | bytes 1572868
  1.4 175.8 %all-to-all-start.2 = ((s32[1,32,1]{2,0,1:T(1,128)}), s32[1,32,1]{2,0,1:T(1,128)S(1)}, u32[]{:S(2)}, u32[]{:S(2)}) async-start(s32[1,32,1]{2,0,1:T(1,128)} %copy.52), calls=%async_computation.2 | async-start | bytes 32768 | tf_op jit(solution)/shard_map/all_to_all | solution.py:59
  12.3 3.9 %copy-start.1 = (bf16[1,512,4096]{2,1,0:T(8,128)(2,1)S(1)}, bf16[1,512,4096]{2,1,0:T(8,128)(2,1)}, u32[]{:S(2)}) copy-start(bf16[1,512,4096]{2,1,0:T(8,128)(2,1)} %param.10) | copy-start | bytes 12582916
  16.1 160.4 %copy-start.4 = (s32[1,32,2]{1,2,0:T(2,128)S(1)}, s32[1,32,2]{1,2,0:T(2,128)}, u32[]{:S(2)}) copy-start(s32[1,32,2]{1,2,0:T(2,128)} %param.15) | copy-start | bytes 772
  16.3 193.3 %copy-start.5 = (u32[256]{0:T(256)S(1)}, u32[256]{0:T(256)}, u32[]{:S(2)}) copy-start(u32[256]{0:T(256)} %constant.72) | copy-start | bytes 3076
  175.8 52.5 %copy-start.3 = (bf16[1,64,4096]{2,1,0:T(8,128)(2,1)S(1)}, bf16[1,64,4096]{2,1,0:T(8,128)(2,1)}, u32[]{:S(2)}) copy-start(bf16[1,64,4096]{2,1,0:T(8,128)(2,1)} %param.14) | copy-start | bytes 1572868
  177.2 25.0 %all-to-all-start.1 = ((s32[1,32,2]{2,0,1:T(1,128)}), s32[1,32,2]{2,0,1:T(1,128)S(1)}, u32[]{:S(2)}, u32[]{:S(2)}) async-start(s32[1,32,2]{2,0,1:T(1,128)} %copy.50), calls=%async_computation.1 | async-start | bytes 32768 | tf_op jit(solution)/shard_map/all_to_all | solution.py:58
  203.7 24.3 %all-to-all-start = ((bf16[32,4,4096]{2,1,0:T(4,128)(2,1)}), bf16[32,4,4096]{2,1,0:T(4,128)(2,1)S(1)}, u32[]{:S(2)}, u32[]{:S(2)}) async-start(bf16[32,4,4096]{2,1,0:T(4,128)(2,1)} %tile.2), calls=%async_computation | async-start | bytes 2097152 | tf_op jit(solution)/shard_map/all_to_all | solution.py:16
